TPU v7x, 32 devices: a whole 2x2x4 slice. The times are simulated.
32 devices in a mesh: grp: 2 (over y), tm: 4 (over x, core), chan: 4 (over z).
Axes of the slice: x: 2, y: 2, z: 4, core: 2. Of those that a mesh axis runs over, the one named last changes fastest.
Arguments:
- records: bfloat16 [512, 3, 1024], P(('grp', 'tm', 'chan')), parts along dimension 0, may hold values from -6 to 6
- templates: bfloat16 [256, 3, 200, 256], P(('tm', 'chan')), may hold values from -6 to 6
- moveouts: int32 [256, 3], P(('tm', 'chan')), may hold values from 0 to 999
- uptime: int32 [512, 2], P(('grp', 'tm', 'chan')), parts along dimension 0, may hold values from 0 to 512
Outputs:
- cccsum: float32 [256, 2048], P(None, ('grp', 'tm', 'chan')), parts along dimension 1
There are 2 independent parts, one for each index of `grp`. A program takes and returns all parts, laid end to end along the dimension named above; an argument that names none is the same for every part. Nothing has to cross between parts.
All inputs are finite; a program needn't handle non-finite values.
Results may differ from a plain program's by a relative error of at most 0.0041.
Values may be sent and summed in bfloat16 or wider, within the bound.
A program may use at most 64 MiB of HBM per device.

v0:
```python
import jax
import jax.numpy as jnp
from jax import lax
from jax.sharding import PartitionSpec as P

MAXMO = 1000


def sender_prep(records, moveouts, uptime):
    stations, components, length = records.shape
    block_count = uptime.shape[1]
    offsets = lax.broadcasted_iota(jnp.int32, (block_count, length // block_count), 1)
    live_mask = (offsets[None, :, :] < uptime[:, :, None]).reshape(stations, 1, length)
    masked = jnp.where(live_mask, records, jnp.zeros((), records.dtype))
    padded = jnp.concatenate(
        [masked, jnp.zeros((stations, components, MAXMO), records.dtype)], axis=2
    )
    flat_rows = padded.reshape(stations * components, length + MAXMO)
    starts = moveouts.reshape(stations * components)

    def slice_row(record_row, start_at):
        return lax.dynamic_slice_in_dim(record_row, start_at, length)

    shifted = jax.vmap(slice_row)(flat_rows, starts)
    return shifted.reshape(stations, components, length)


def normalize_templates(templates):
    values = templates.astype(jnp.float32)
    squares = jnp.sum(values * values, axis=2, keepdims=True)
    return (values * lax.rsqrt(squares + 1e-06)).astype(jnp.bfloat16)


def correlate_station(station_rows, unit_rows):
    channels, length = station_rows.shape
    window_len = unit_rows.shape[1]
    out_len = length - window_len + 1
    tiled_rows = jnp.tile(station_rows, (1, window_len + 1))[:, : window_len * (length + 1)]
    windows = tiled_rows.reshape(channels, window_len, length + 1)[:, :, :out_len]
    energy = jnp.sum(jnp.square(windows.astype(jnp.float32)), axis=1)
    factor = lax.rsqrt(jnp.maximum(energy, 1.0))
    scaled = (windows.astype(jnp.float32) * factor[:, None, :]).astype(jnp.bfloat16)
    unit_flat = unit_rows.reshape(channels * window_len, unit_rows.shape[2])
    return jnp.dot(
        unit_flat.T,
        scaled.reshape(channels * window_len, out_len),
        preferred_element_type=jnp.float32,
    )


def margin_blocks(signal, block_len, window_len):
    lead_shape = signal.shape[:-1]
    length = signal.shape[-1]
    block_count = length // block_len
    padded = jnp.concatenate([signal, jnp.zeros(lead_shape + (block_len,), signal.dtype)], axis=-1)
    grid = padded.reshape(lead_shape + (block_count + 1, block_len))
    main_part = grid[..., :block_count, :]
    rim_part = grid[..., 1:, : window_len - 1]
    return jnp.concatenate([main_part, rim_part], axis=-1)


def body(records, templates, moveouts, uptime):
    shifted = sender_prep(records, moveouts, uptime)
    unit_bank = normalize_templates(templates)
    window_len = unit_bank.shape[2]
    time_groups = lax.axis_size("tm")
    blocks = margin_blocks(shifted, shifted.shape[2] // time_groups, window_len)
    extended = lax.all_to_all(blocks, "tm", split_axis=2, concat_axis=0, tiled=True)[:, :, 0, :]
    initial = jnp.zeros((unit_bank.shape[3], extended.shape[2] - window_len + 1), jnp.float32)
    piece_rows = lax.all_gather(unit_bank, "tm", axis=0, tiled=True)

    def one_station(station, running_sum):
        station_rows = lax.dynamic_index_in_dim(extended, station, 0, keepdims=False)
        unit_rows = lax.dynamic_index_in_dim(piece_rows, station, 0, keepdims=False)
        return running_sum + correlate_station(station_rows, unit_rows)

    partial_value = lax.fori_loop(0, piece_rows.shape[0], one_station, initial)
    return lax.psum_scatter(partial_value, "chan", scatter_dimension=1, tiled=True)


def solution(mesh):
    placed = (
        P(("grp", "tm", "chan"), None, None),
        P(("tm", "chan"), None, None, None),
        P(("tm", "chan"), None),
        P(("grp", "tm", "chan"), None),
    )
    return jax.shard_map(
        body, mesh=mesh, in_specs=placed, out_specs=P(None, ("grp", "tm", "chan")), check_vma=False
    )
```

profile of v0, /device:TPU:0, one launch (start us, length us, event | category | flops | bytes accessed | tf_op | source)
XLA Modules:
  0.0 491.2 jit_solution(4632010004564827906)
XLA Ops:
  6.5 3.5 fusion.2
  10.1 5.8 %fusion.3 = bf16[16,3,200,256]{3,2,1,0:T(8,128)(2,1)} fusion(bf16[16,3,200,256]{3,2,1,0:T(8,128)(2,1)} %param.7, f32[16,3,256]{2,1,0:T(4,128)S(1)} %add_rsqrt_fusion), kind=kLoop, calls=%fused_computation.12 | loop fusion | flops 7372800 | bytes 9879552 | tf_op jit(solution)/shard_map/convert_element_type | solution.py:31
  16.8 99.4 %while.15 = (s32[]{:T(128)}, bf16[48,2024]{1,0:T(8,128)(2,1)S(1)}, s32[48,2]{0,1:T(2,128)S(1)}, bf16[48,1024]{1,0:T(8,128)(2,1)S(1)}, s32[]{:T(128)}, /*index=5*/s32[]{:T(128)}) while((s32[]{:T(128)}, bf16[48,2024]{1,0:T(8,128)(2,1)S(1)}, s32[48,2]{0,1:T(2,128)S(1)}, bf16[48,1024]{1,0:T(8,128)(2,1)S(1)}, s32[]{:T(128)}, /*index=5*/s32[]{:T(128)}) %tuple.49), condition=%wide.while_cond, body=%wide.while_body.sunk | while | flops 2 | bytes 8305 | solution.py:22
  117.4 4.2 all-to-all-start
  121.6 7.9 %all-to-all-done = bf16[16,3,4,455]{3,0,1,2:T(8,128)(2,1)S(1)} async-done(((bf16[16,3,4,455]{3,0,1,2:T(8,128)(2,1)}), bf16[16,3,4,455]{3,0,1,2:T(8,128)(2,1)S(1)}, u32[]{:S(2)}, u32[]{:S(2)}) %all-to-all-start) | async-done | bytes 174752 | tf_op jit(solution)/shard_map/all_to_all | solution.py:68
  129.7 15.5 %all-gather.2.cloned.1.call-done = bf16[64,3,200,256]{3,2,1,0:T(8,128)(2,1)} async-done(((bf16[16,3,200,256]{3,2,1,0:T(8,128)(2,1)}), bf16[64,3,200,256]{3,2,1,0:T(8,128)(2,1)}) %all-gather.2.cloned.1.call-update) | async-done | bytes 19660816 | tf_op jit(solution)/shard_map/all_gather | solution.py:70
  145.2 318.2 %while.16 = (s32[]{:T(128)}, f32[256,256]{1,0:T(8,128)S(1)}, bf16[64,3,200,256]{3,2,1,0:T(8,128)(2,1)}, bf16[64,3,455]{2,1,0:T(4,128)(2,1)S(1)}, s32[]{:T(128)}, /*index=5*/s32[]{:T(128)}) while((s32[]{:T(128)}, f32[256,256]{1,0:T(8,128)S(1)}, bf16[64,3,200,256]{3,2,1,0:T(8,128)(2,1)}, bf16[64,3,455]{2,1,0:T(4,128)(2,1)S(1)}, ...), condition=%wide.region_3.4_spmd.clone, body=%wide.region_1.3_spmd.clone.sunk | while | flops 79695872 | bytes 6530243 | solution.py:77
  145.3 1.6 tile.29
  150.3 1.6 tile.29
  155.2 1.6 tile.29
  160.2 1.6 tile.29
  165.2 1.6 tile.29
  175.1 1.6 tile.29
  180.1 1.6 tile.29
  185.1 1.6 tile.29
  190.0 1.6 tile.29
  195.0 1.6 tile.29
  204.9 1.6 tile.29
  209.9 1.6 tile.29
  214.9 1.6 tile.29
  219.9 1.6 tile.29
  224.8 1.6 tile.29
  234.8 1.6 tile.29
  464.3 20.1 %reduce-scatter.2.cloned.1.call-done = f32[256,64]{0,1:T(8,128)} async-done(((f32[256,256]{0,1:T(8,128)}), f32[256,64]{0,1:T(8,128)}) %reduce-scatter.2.cloned.1.call-update) | async-done | bytes 65552 | tf_op jit(solution)/shard_map/reduce_scatter | solution.py:78
  (855 shorter events, 389.1 us)
Async XLA Ops:
  6.5 9.4 %copy-start.2 = (s32[16,2]{0,1:T(2,128)S(1)}, s32[16,2]{0,1:T(2,128)}, u32[]{:S(2)}) copy-start(s32[16,2]{0,1:T(2,128)} %param.9) | copy-start | bytes 388
  6.5 9.6 %copy-start = (bf16[16,3,1024]{2,0,1:T(8,128)(2,1)S(1)}, bf16[16,3,1024]{2,0,1:T(8,128)(2,1)}, u32[]{:S(2)}) copy-start(bf16[16,3,1024]{2,0,1:T(8,128)(2,1)} %param.6) | copy-start | bytes 294916
  6.5 10.0 %copy-start.1 = (s32[16,3]{0,1:T(4,128)S(1)}, s32[16,3]{0,1:T(4,128)}, u32[]{:S(2)}) copy-start(s32[16,3]{0,1:T(4,128)} %param.8) | copy-start | bytes 580
  6.5 138.7 %all-gather.2.cloned.1.call-start = ((), (), s32[]{:S(2)}) async-start(), calls=%async_computation.2 | async-start | bytes 24576000 | tf_op jit(solution)/shard_map/all_gather | solution.py:70
  117.4 12.1 %all-to-all-start = ((bf16[16,3,4,455]{3,0,1,2:T(8,128)(2,1)}), bf16[16,3,4,455]{3,0,1,2:T(8,128)(2,1)S(1)}, u32[]{:S(2)}, u32[]{:S(2)}) async-start(bf16[16,3,4,455]{3,0,1,2:T(8,128)(2,1)} %copy.33), calls=%async_computation | async-start | bytes 393216 | tf_op jit(solution)/shard_map/all_to_all | solution.py:68
  121.6 362.7 %reduce-scatter.2.cloned.1.call-start = ((), (), s32[]{:S(2)}) async-start(), calls=%async_computation.3 | async-start | bytes 327680 | tf_op jit(solution)/shard_map/reduce_scatter | solution.py:78
Sparse Core Ops, SparseCore 0:
  16.0 129.1 all-gather.1
  464.4 19.9 reduce-scatter.1
where the time goes:
time: 495 us; the launch traced here: 491 us
  local copies, waits for them, and re-layouts  382 us (77%)
  waiting for transfers between devices  43.6 us (9%)
  matrix products  22.9 us (5%)
  other arithmetic  19 us (4%)
  between operations  13.6 us (3%)
  loops' own time  6.32 us (1%)
    another operation x192, local copies, waits for them, and re-layouts, correlate_station(): jnp.tile(station_rows, (1, window_len + 1))[:, :window_len * (length + 1)]  104 us
    gather x192, local copies, waits for them, and re-layouts  98.2 us
    reshape x64, local copies, waits for them, and re-layouts, correlate_station(): tiled_rows.reshape(channels, window_len, length + 1)[:, :, :out_len]  96.7 us
    dynamic_slice x64, local copies, waits for them, and re-layouts, one_station(): unit_rows = lax.dynamic_index_in_dim(piece_rows, station, 0, keepdims=False)  63.6 us
    dot_general x64, matrix products, correlate_station(): jnp.dot(unit_flat.T, scaled.reshape(channels * window_len, out_len), pref...  22.9 us
    reduce_scatter x1, waiting for transfers between devices, body(): lax.psum_scatter(partial_value, 'chan', scatter_dimension=1, tiled=True)  20.1 us
    slice x64, local copies, waits for them, and re-layouts, correlate_station(): jnp.tile(station_rows, (1, window_len + 1))[:, :window_len * (length + 1)]  16.2 us
    all_gather x1, waiting for transfers between devices, body(): piece_rows = lax.all_gather(unit_bank, 'tm', axis=0, tiled=True)  15.5 us
  transfers between devices with their start and end apart: 3, of which 3 were waited for; matrix products, arithmetic and copies ran while one was open for 20% of the time, Pallas kernels for 0%

commit v1 on v0

v1 whole, which is shorter than its diff:
```python
import functools

import jax
import jax.numpy as jnp
from jax import lax
from jax.experimental import pallas as pl
from jax.experimental.pallas import tpu as pltpu
from jax.sharding import PartitionSpec as P

LANES = 128
SUBS = 8


def roll_left(value, amount):
    size = value.shape[-1]
    return pltpu.roll(value, (size - amount) % size, axis=1)


def windowed_sum(squares, window_len):
    total, covered, power, width = None, 0, squares, 1
    while width <= window_len:
        if window_len & width:
            piece = power if covered == 0 else roll_left(power, covered)
            total = piece if total is None else total + piece
            covered += width
        if 2 * width <= window_len:
            power = power + roll_left(power, width)
        width *= 2
    return total


def correlate_kernel(moveouts, uptime, records, templates, out, rows, windows, units, total):
    step = pl.program_id(0)
    _, components, length = records.shape
    window_len = templates.shape[2]
    depth = units.shape[0] // components
    padded = rows.shape[1]
    block_count = uptime.shape[1]
    block_len = length // block_count

    @pl.when(step == 0)
    def _():
        rows[...] = jnp.zeros_like(rows)
        units[...] = jnp.zeros_like(units)
        total[...] = jnp.zeros_like(total)

    time = lax.broadcasted_iota(jnp.int32, (1, length), 1)
    limit = jnp.zeros((1, length), jnp.int32)
    for block in range(block_count):
        limit = jnp.where(time >= block * block_len, block * block_len + uptime[step, block], limit)
    for comp in range(components):
        row = records[0, comp:comp + 1, :].astype(jnp.float32)
        row = jnp.where(time < limit, row, 0.0)
        start = moveouts[step, comp]
        row = pltpu.roll(row, lax.rem(length - start, length), axis=1)
        rows[comp:comp + 1, :length] = jnp.where(time < length - start, row, 0.0)

    signal = rows[...]
    energy = windowed_sum(signal * signal, window_len)
    factor = lax.rsqrt(jnp.maximum(energy[:, :length], 1.0)).T

    sub = lax.broadcasted_iota(jnp.int32, (SUBS, padded), 0)
    for comp in range(components):
        values = templates[0, comp].astype(jnp.float32)
        squares = jnp.sum(values * values, axis=0, keepdims=True)
        unit = (values * lax.rsqrt(squares + 1e-06)).astype(jnp.bfloat16)
        units[comp * depth:comp * depth + window_len, :] = unit

        base = jnp.broadcast_to(rows[comp:comp + 1, :], (SUBS, padded))
        for bit in (1, 2, 4):
            base = jnp.where((sub & bit) != 0, roll_left(base, bit), base)
        for pair in range(LANES // (2 * SUBS)):
            first = base if pair == 0 else roll_left(base, 2 * SUBS * pair)
            second = roll_left(base, 2 * SUBS * pair + SUBS)
            both = jnp.concatenate([first, second], axis=0)
            for chunk in range(length // LANES):
                top = chunk * LANES + 2 * SUBS * pair
                scale = factor[top:top + 2 * SUBS, comp:comp + 1]
                window = both[:, chunk * LANES:chunk * LANES + depth]
                windows[top:top + 2 * SUBS, comp * depth:(comp + 1) * depth] = (
                    window * scale
                ).astype(jnp.bfloat16)

    total[...] += jnp.dot(windows[...], units[...], preferred_element_type=jnp.float32)

    @pl.when(step == pl.num_programs(0) - 1)
    def _():
        out[...] = total[...].astype(out.dtype)


def correlate(records, templates, moveouts, uptime):
    stations, components, length = records.shape
    _, _, window_len, bank = templates.shape
    depth = pl.cdiv(window_len, LANES) * LANES
    padded = length + depth
    return pl.pallas_call(
        correlate_kernel,
        out_shape=jax.ShapeDtypeStruct((length, bank), jnp.float32),
        grid_spec=pltpu.PrefetchScalarGridSpec(
            num_scalar_prefetch=2,
            grid=(stations,),
            in_specs=[
                pl.BlockSpec((1, components, length), lambda s, *_: (s, 0, 0)),
                pl.BlockSpec((1, components, window_len, bank), lambda s, *_: (s, 0, 0, 0)),
            ],
            out_specs=pl.BlockSpec((length, bank), lambda s, *_: (0, 0)),
            scratch_shapes=[
                pltpu.VMEM((SUBS, padded), jnp.float32),
                pltpu.VMEM((length, components * depth), jnp.bfloat16),
                pltpu.VMEM((components * depth, bank), jnp.bfloat16),
                pltpu.VMEM((length, bank), jnp.float32),
            ],
        ),
        name="correlate",
    )(moveouts, uptime, records, templates)


def body(records, templates, moveouts, uptime):
    partial = correlate(records, templates, moveouts, uptime)
    mine = lax.psum_scatter(partial, ("tm", "chan"), scatter_dimension=0, tiled=True)
    return mine.T


def solution(mesh):
    placed = (
        P(("grp", "tm", "chan"), None, None),
        P(("tm", "chan"), None, None, None),
        P(("tm", "chan"), None),
        P(("grp", "tm", "chan"), None),
    )
    return jax.shard_map(
        body, mesh=mesh, in_specs=placed, out_specs=P(None, ("grp", "tm", "chan")), check_vma=False
    )
```

time: 495 us -> 121 us (0.24)
  local copies, waits for them, and re-layouts: 382 us -> 4.33 us
  Pallas kernels: 0 us -> 42.6 us
  matrix products: 22.9 us -> 0 us
  other arithmetic: 19 us -> 0 us
  waiting for transfers between devices: 43.6 us -> 60.5 us
  loops' own time: 6.32 us -> 0 us
    another operation x192 -> x0, local copies, waits for them, and re-layouts: 104 us -> none  [correlate_station(): jnp.tile(station_rows, (1, window_len + 1))[:, :window_len * (length + 1)]]
    gather x192 -> x0, local copies, waits for them, and re-layouts: 98.2 us -> none
    reshape x68 -> x0, local copies, waits for them, and re-layouts: 97.2 us -> none  [the longest x64 96.7 us: correlate_station(): tiled_rows.reshape(channels, window_len, length + 1)[:, :, :out_len]]
    dynamic_slice x64 -> x0, local copies, waits for them, and re-layouts: 63.6 us -> none  [one_station(): unit_rows = lax.dynamic_index_in_dim(piece_rows, station, 0, keepdims=False)]
    pallas_call x0 -> x1, Pallas kernels: none -> 42.6 us  [correlate(): pl.pallas_call(correlate_kernel, out_shape=jax.ShapeDtypeStruct((length,...]
    reduce_scatter x1, waiting for transfers between devices: 20.1 us -> 60.4 us  [body(): lax.psum_scatter(partial, ('tm', 'chan'), scatter_dimension=0, tiled=True)]
    dot_general x64 -> x0, matrix products: 22.9 us -> none  [correlate_station(): jnp.dot(unit_flat.T, scaled.reshape(channels * window_len, out_len), pref...]
    slice x66 -> x0, local copies, waits for them, and re-layouts: 16.3 us -> none  [the longest x64 16.2 us: correlate_station(): jnp.tile(station_rows, (1, window_len + 1))[:, :window_len * (length + 1)]]
  transfers between devices with their start and end apart: 3 -> 1, of which waited for: 3 -> 1; matrix products, arithmetic and copies ran while one was open for 20% -> 0% of each run, Pallas kernels for 0% -> 0%
where the time goes in v1:
time: 121 us
  waiting for transfers between devices  60.5 us (50%)
  Pallas kernels  42.6 us (35%)
  between operations  13.4 us (11%)
  local copies, waits for them, and re-layouts  4.33 us (4%)
    reduce_scatter x1, waiting for transfers between devices, body(): lax.psum_scatter(partial, ('tm', 'chan'), scatter_dimension=0, tiled=True)  60.4 us
    pallas_call x1, Pallas kernels, correlate(): pl.pallas_call(correlate_kernel, out_shape=jax.ShapeDtypeStruct((length,...  42.6 us
    unnamed x3, local copies, waits for them, and re-layouts  4.33 us
  transfers between devices with their start and end apart: 1, of which 1 were waited for; matrix products, arithmetic and copies ran while one was open for 0% of the time, Pallas kernels for 0%

profile of v1, /device:TPU:0, one launch (start us, length us, event | category | flops | bytes accessed | tf_op | source)
XLA Modules:
  0.0 120.8 jit_solution(15864019918768824797)
XLA Ops:
  6.5 0.0 reduce-scatter.2.cloned.1.call-start
  6.5 1.4 %copy.5.moveouts = s32[16,3]{1,0:T(8,128)} copy(s32[16,3]{0,1:T(4,128)} %param.6) | data formatting | bytes 384 | tf_op args[2]
  7.9 1.3 %copy.6.uptime = s32[16,2]{1,0:T(8,128)} copy(s32[16,2]{0,1:T(2,128)} %param.7) | data formatting | bytes 256 | tf_op args[3]
  9.2 1.6 %copy.7.records = bf16[16,3,1024]{2,1,0:T(4,128)(2,1)} copy(bf16[16,3,1024]{2,0,1:T(8,128)(2,1)} %param.4) | data formatting | bytes 196608 | tf_op args[0]
  10.9 42.6 %correlate.1 = f32[1024,256]{1,0:T(8,128)} custom-call(s32[16,3]{1,0:T(8,128)} %copy.5.moveouts, s32[16,2]{1,0:T(8,128)} %copy.6.uptime, bf16[16,3,1024]{2,1,0:T(4,128)(2,1)} %copy.7.records, bf16[16,3,200,256]{3,2,1,0:T(8,128)(2,1)} %templates.1), custom_call_target="tpu_custom_call" | custom-call | tf_op jit(solution)/shard_map/correlate/pallas_call | solution.py:96
  53.5 0.0 reduce-scatter.2.cloned.1.call-update
  53.5 60.4 %reduce-scatter.2.cloned.1.call-done = f32[64,256]{1,0:T(8,128)} async-done(((f32[1024,256]{1,0:T(8,128)}), f32[64,256]{1,0:T(8,128)}) %reduce-scatter.2.cloned.1.call-update) | async-done | bytes 65552 | tf_op jit(solution)/shard_map/reduce_scatter | solution.py:120
Async XLA Ops:
  6.5 107.4 %reduce-scatter.2.cloned.1.call-start = ((), (), s32[]{:S(2)}) async-start(), calls=%async_computation.1 | async-start | bytes 1114112 | tf_op jit(solution)/shard_map/reduce_scatter | solution.py:120
Sparse Core Ops, SparseCore 0:
  53.6 60.2 reduce-scatter.1

commit v2 on v1

--- a/solution.py
+++ b/solution.py
@@ -29,29 +29,28 @@
     return total
 
 
-def correlate_kernel(moveouts, uptime, records, templates, out, rows, windows, units, total):
+def correlate_kernel(blocks, counts, records, templates, out, traces, rows, windows, units, total):
     step = pl.program_id(0)
-    _, components, length = records.shape
+    components, _, length = records.shape
     window_len = templates.shape[2]
     depth = units.shape[0] // components
     padded = rows.shape[1]
-    block_count = uptime.shape[1]
-    block_len = length // block_count
+    block_len = length // blocks
 
     @pl.when(step == 0)
     def _():
+        traces[...] = records[...].astype(jnp.float32)
         rows[...] = jnp.zeros_like(rows)
         units[...] = jnp.zeros_like(units)
         total[...] = jnp.zeros_like(total)
 
     time = lax.broadcasted_iota(jnp.int32, (1, length), 1)
     limit = jnp.zeros((1, length), jnp.int32)
-    for block in range(block_count):
-        limit = jnp.where(time >= block * block_len, block * block_len + uptime[step, block], limit)
+    for block in range(blocks):
+        limit = jnp.where(time >= block * block_len, block * block_len + counts[components + block, step], limit)
     for comp in range(components):
-        row = records[0, comp:comp + 1, :].astype(jnp.float32)
-        row = jnp.where(time < limit, row, 0.0)
-        start = moveouts[step, comp]
+        row = jnp.where(time < limit, traces[comp, pl.ds(step, 1), :], 0.0)
+        start = counts[comp, step]
         row = pltpu.roll(row, lax.rem(length - start, length), axis=1)
         rows[comp:comp + 1, :length] = jnp.where(time < length - start, row, 0.0)
 
@@ -93,18 +92,20 @@
     _, _, window_len, bank = templates.shape
     depth = pl.cdiv(window_len, LANES) * LANES
     padded = length + depth
+    counts = jnp.concatenate([moveouts.T, uptime.T], axis=0)
     return pl.pallas_call(
-        correlate_kernel,
+        functools.partial(correlate_kernel, uptime.shape[1]),
         out_shape=jax.ShapeDtypeStruct((length, bank), jnp.float32),
         grid_spec=pltpu.PrefetchScalarGridSpec(
-            num_scalar_prefetch=2,
+            num_scalar_prefetch=1,
             grid=(stations,),
             in_specs=[
-                pl.BlockSpec((1, components, length), lambda s, *_: (s, 0, 0)),
+                pl.BlockSpec((components, stations, length), lambda s, *_: (0, 0, 0)),
                 pl.BlockSpec((1, components, window_len, bank), lambda s, *_: (s, 0, 0, 0)),
             ],
             out_specs=pl.BlockSpec((length, bank), lambda s, *_: (0, 0)),
             scratch_shapes=[
+                pltpu.VMEM((components, stations, length), jnp.float32),
                 pltpu.VMEM((SUBS, padded), jnp.float32),
                 pltpu.VMEM((length, components * depth), jnp.bfloat16),
                 pltpu.VMEM((components * depth, bank), jnp.bfloat16),
@@ -112,13 +113,115 @@
             ],
         ),
         name="correlate",
-    )(moveouts, uptime, records, templates)
+    )(counts, records.transpose(1, 0, 2), templates)
+
+
+def reduce_kernel(
+    x_size, z_size, part, out, from_core, to_x, from_x, to_z, from_z,
+    core_send, core_recv, x_send, x_recv, z_send, z_recv,
+):
+    tm, z = lax.axis_index("tm"), lax.axis_index("chan")
+    x, core = lax.div(tm, 2), lax.rem(tm, 2)
+    rows = part.shape[0] // (2 * x_size)
+    piece = rows // z_size
+    mesh_id = pl.DeviceIdType.MESH
+    partner = 1 - core + 2 * x
+
+    barrier = pltpu.get_barrier_semaphore()
+    pl.semaphore_signal(barrier, inc=1, device_id={"tm": partner}, device_id_type=mesh_id)
+    for d in range(1, x_size):
+        peer = 2 * lax.rem(x + d, x_size) + core
+        pl.semaphore_signal(barrier, inc=1, device_id={"tm": peer}, device_id_type=mesh_id)
+    for e in range(1, z_size):
+        peer = lax.rem(z + e, z_size)
+        pl.semaphore_signal(barrier, inc=1, device_id={"chan": peer}, device_id_type=mesh_id)
+    pl.semaphore_wait(barrier, x_size + z_size - 1)
+
+    def start(src, dst, send, recv, device):
+        copy = pltpu.make_async_remote_copy(
+            src_ref=src, dst_ref=dst, send_sem=send, recv_sem=recv,
+            device_id=device, device_id_type=mesh_id,
+        )
+        copy.start()
+        return copy
+
+    core_copies, x_copies, z_copies = [], [], []
+    for d in range(1, x_size + 1):
+        peer = lax.rem(x + d, x_size)
+        first = pl.multiple_of((2 * peer + 1 - core) * rows, rows)
+        core_copies.append(start(
+            part.at[pl.ds(first, rows)], from_core.at[d - 1],
+            core_send.at[d - 1], core_recv.at[d - 1], {"tm": partner},
+        ))
+
+    for d in range(1, x_size):
+        peer = lax.rem(x + d, x_size)
+        core_copies[d - 1].wait_recv()
+        pending = []
+        for e in range(1, z_size + 1):
+            offset = pl.multiple_of(lax.rem(z + e, z_size) * piece, piece)
+            first = pl.multiple_of((2 * peer + core) * rows + offset, piece)
+            value = part[pl.ds(first, piece), :] + from_core[d - 1, pl.ds(offset, piece), :]
+            to_x[d - 1, pl.ds(offset, piece), :] = value.astype(to_x.dtype)
+            pending.append(start(
+                to_x.at[d - 1, pl.ds(offset, piece)], from_x.at[d - 1, pl.ds(offset, piece)],
+                x_send.at[d - 1, e - 1], x_recv.at[d - 1, e - 1], {"tm": 2 * peer + core},
+            ))
+        x_copies.append(pending)
+
+    core_copies[x_size - 1].wait_recv()
+    for e in range(1, z_size + 1):
+        peer = lax.rem(z + e, z_size)
+        offset = pl.multiple_of(peer * piece, piece)
+        first = pl.multiple_of(tm * rows + offset, piece)
+        value = part[pl.ds(first, piece), :] + from_core[x_size - 1, pl.ds(offset, piece), :]
+        for d in range(1, x_size):
+            x_copies[d - 1][e - 1].wait_recv()
+            value = value + from_x[d - 1, pl.ds(offset, piece), :].astype(jnp.float32)
+        if e < z_size:
+            to_z[e - 1] = value.astype(to_z.dtype)
+            z_copies.append(start(
+                to_z.at[e - 1], from_z.at[e - 1], z_send.at[e - 1], z_recv.at[e - 1],
+                {"chan": peer},
+            ))
+    for e in range(1, z_size):
+        z_copies[e - 1].wait_recv()
+        value = value + from_z[e - 1].astype(jnp.float32)
+    out[...] = value
+
+    for copy in core_copies + [c for pending in x_copies for c in pending] + z_copies:
+        copy.wait_send()
+
+
+def reduce_scatter(part):
+    x_size, z_size = lax.axis_size("tm") // 2, lax.axis_size("chan")
+    length, bank = part.shape
+    rows = length // (2 * x_size)
+    piece = rows // z_size
+    others_x, others_z = max(x_size - 1, 1), max(z_size - 1, 1)
+    dma = pltpu.SemaphoreType.DMA
+    return pl.pallas_call(
+        functools.partial(reduce_kernel, x_size, z_size),
+        out_shape=jax.ShapeDtypeStruct((piece, bank), jnp.float32),
+        in_specs=[pl.BlockSpec(memory_space=pltpu.VMEM)],
+        out_specs=pl.BlockSpec(memory_space=pltpu.VMEM),
+        scratch_shapes=[
+            pltpu.VMEM((x_size, rows, bank), jnp.float32),
+            pltpu.VMEM((others_x, rows, bank), jnp.bfloat16),
+            pltpu.VMEM((others_x, rows, bank), jnp.bfloat16),
+            pltpu.VMEM((others_z, piece, bank), jnp.bfloat16),
+            pltpu.VMEM((others_z, piece, bank), jnp.bfloat16),
+            dma((x_size,)), dma((x_size,)),
+            dma((others_x, z_size)), dma((others_x, z_size)),
+            dma((others_z,)), dma((others_z,)),
+        ],
+        compiler_params=pltpu.CompilerParams(collective_id=0, has_side_effects=True),
+        name="reduce_scatter",
+    )(part)
 
 
 def body(records, templates, moveouts, uptime):
-    partial = correlate(records, templates, moveouts, uptime)
-    mine = lax.psum_scatter(partial, ("tm", "chan"), scatter_dimension=0, tiled=True)
-    return mine.T
+    return reduce_scatter(correlate(records, templates, moveouts, uptime)).T
 
 
 def solution(mesh):

time: 121 us -> 61.1 us (0.50)
  waiting for transfers between devices: 60.5 us -> 0 us
  Pallas kernels: 42.6 us -> 58.1 us
  between operations: 13.4 us -> 0.01 us
  local copies, waits for them, and re-layouts: 4.33 us -> 1.47 us
  other arithmetic: 0 us -> 1.3 us
    reduce_scatter x1 -> x0, waiting for transfers between devices: 60.4 us -> none  [body(): lax.psum_scatter(partial, ('tm', 'chan'), scatter_dimension=0, tiled=True)]
    pallas_call x1 -> x2, Pallas kernels: 42.6 us -> 58.1 us  [the longest x1 42.2 us: correlate(): pl.pallas_call(functools.partial(correlate_kernel, uptime.shape[1]), out_...]
    unnamed x3 -> x1, local copies, waits for them, and re-layouts: 4.33 us -> 1.47 us
    concatenate x0 -> x1, other arithmetic: none -> 1.3 us  [correlate(): counts = jnp.concatenate([moveouts.T, uptime.T], axis=0)]
  transfers between devices with their start and end apart: 1 -> 0, of which waited for: 1 -> 0; matrix products, arithmetic and copies ran while one was open for 0% -> 0% of each run, Pallas kernels for 0% -> 0%
where the time goes in v2:
time: 61.1 us; the launch traced here: 60.8 us
  Pallas kernels  58.1 us (95%)
  local copies, waits for them, and re-layouts  1.47 us (2%)
  other arithmetic  1.3 us (2%)
    pallas_call x1, Pallas kernels, correlate(): pl.pallas_call(functools.partial(correlate_kernel, uptime.shape[1]), out_...  42.2 us
    pallas_call x1, Pallas kernels, reduce_scatter(): pl.pallas_call(functools.partial(reduce_kernel, x_size, z_size), out_shap...  15.8 us
    unnamed x1, local copies, waits for them, and re-layouts  1.47 us
    concatenate x1, other arithmetic, correlate(): counts = jnp.concatenate([moveouts.T, uptime.T], axis=0)  1.3 us

profile of v2, /device:TPU:0, one launch (start us, length us, event | category | flops | bytes accessed | tf_op | source)
XLA Modules:
  0.0 60.8 jit_solution(15071034034618792601)
XLA Ops:
  0.0 1.3 %pad_add_fusion.counts = s32[5,16]{1,0:T(8,128)} fusion(s32[2,16]{1,0:T(2,128)} %bitcast.7, s32[3,16]{1,0:T(4,128)} %bitcast.6), kind=kLoop, calls=%fused_computation | loop fusion | flops 80 | bytes 640 | tf_op jit(solution)/shard_map/concatenate | solution.py:95
  1.3 42.2 %correlate.1.part = f32[1024,256]{1,0:T(8,128)} custom-call(s32[5,16]{1,0:T(8,128)} %pad_add_fusion.counts, bf16[3,16,1024]{2,1,0:T(8,128)(2,1)} %bitcast.5, bf16[16,3,200,256]{3,2,1,0:T(8,128)(2,1)} %templates.1), custom_call_target="tpu_custom_call" | custom-call | tf_op jit(solution)/shard_map/correlate/pallas_call | solution.py:96
  43.5 15.8 %reduce_scatter.1 = f32[64,256]{1,0:T(8,128)} custom-call(f32[1024,256]{1,0:T(8,128)} %correlate.1.part), custom_call_target="tpu_custom_call" | custom-call | tf_op jit(solution)/shard_map/reduce_scatter/pallas_call | solution.py:203
  59.4 1.5 %copy.6 = f32[256,64]{0,1:T(8,128)} copy(f32[256,64]{0,1:T(8,128)} %bitcast.4) | data formatting | bytes 131072

commit v3 on v2

--- a/solution.py
+++ b/solution.py
@@ -9,6 +9,7 @@
 
 LANES = 128
 SUBS = 8
+ROT = jnp.bfloat16
 
 
 def roll_left(value, amount):
@@ -33,7 +34,7 @@
     step = pl.program_id(0)
     components, _, length = records.shape
     window_len = templates.shape[2]
-    depth = units.shape[0] // components
+    depth = units.shape[1] // components
     padded = rows.shape[1]
     block_len = length // blocks
 
@@ -41,7 +42,7 @@
     def _():
         traces[...] = records[...].astype(jnp.float32)
         rows[...] = jnp.zeros_like(rows)
-        units[...] = jnp.zeros_like(units)
+        windows[...] = jnp.zeros_like(windows)
         total[...] = jnp.zeros_like(total)
 
     time = lax.broadcasted_iota(jnp.int32, (1, length), 1)
@@ -56,35 +57,35 @@
 
     signal = rows[...]
     energy = windowed_sum(signal * signal, window_len)
-    factor = lax.rsqrt(jnp.maximum(energy[:, :length], 1.0)).T
+    factor = lax.rsqrt(jnp.maximum(energy[:, :length], 1.0))
 
     sub = lax.broadcasted_iota(jnp.int32, (SUBS, padded), 0)
     for comp in range(components):
         values = templates[0, comp].astype(jnp.float32)
         squares = jnp.sum(values * values, axis=0, keepdims=True)
         unit = (values * lax.rsqrt(squares + 1e-06)).astype(jnp.bfloat16)
-        units[comp * depth:comp * depth + window_len, :] = unit
+        blank = jnp.zeros((depth - window_len, unit.shape[1]), unit.dtype)
+        units[:, comp * depth:(comp + 1) * depth] = jnp.concatenate([unit, blank], axis=0).T
 
         base = jnp.broadcast_to(rows[comp:comp + 1, :], (SUBS, padded))
         for bit in (1, 2, 4):
             base = jnp.where((sub & bit) != 0, roll_left(base, bit), base)
-        for pair in range(LANES // (2 * SUBS)):
-            first = base if pair == 0 else roll_left(base, 2 * SUBS * pair)
-            second = roll_left(base, 2 * SUBS * pair + SUBS)
-            both = jnp.concatenate([first, second], axis=0)
-            for chunk in range(length // LANES):
-                top = chunk * LANES + 2 * SUBS * pair
-                scale = factor[top:top + 2 * SUBS, comp:comp + 1]
-                window = both[:, chunk * LANES:chunk * LANES + depth]
-                windows[top:top + 2 * SUBS, comp * depth:(comp + 1) * depth] = (
-                    window * scale
+        both = jnp.concatenate([base, roll_left(base, SUBS)], axis=0).astype(ROT)
+        scale = jnp.broadcast_to(factor[comp:comp + 1, :], (2 * SUBS, length))
+        for group in range(LANES // (2 * SUBS)):
+            shifted = both if group == 0 else roll_left(both, 2 * SUBS * group)
+            shifted = shifted.astype(jnp.float32)
+            for lag in range(2 * SUBS * group, window_len, LANES):
+                skip = lag // LANES * LANES
+                windows[comp * depth + lag:comp * depth + lag + 2 * SUBS, :] = (
+                    shifted[:, skip:skip + length] * scale
                 ).astype(jnp.bfloat16)
 
-    total[...] += jnp.dot(windows[...], units[...], preferred_element_type=jnp.float32)
+    total[...] += jnp.dot(units[...], windows[...], preferred_element_type=jnp.float32)
 
     @pl.when(step == pl.num_programs(0) - 1)
     def _():
-        out[...] = total[...].astype(out.dtype)
+        out[...] = total[...].T
 
 
 def correlate(records, templates, moveouts, uptime):
@@ -107,9 +108,9 @@
             scratch_shapes=[
                 pltpu.VMEM((components, stations, length), jnp.float32),
                 pltpu.VMEM((SUBS, padded), jnp.float32),
-                pltpu.VMEM((length, components * depth), jnp.bfloat16),
-                pltpu.VMEM((components * depth, bank), jnp.bfloat16),
-                pltpu.VMEM((length, bank), jnp.float32),
+                pltpu.VMEM((components * depth, length), jnp.bfloat16),
+                pltpu.VMEM((bank, components * depth), jnp.bfloat16),
+                pltpu.VMEM((bank, length), jnp.float32),
             ],
         ),
         name="correlate",

time: 61.1 us -> 52.9 us (0.87)
  Pallas kernels: 58.1 us -> 49.9 us
    pallas_call x1, Pallas kernels: 42.2 us -> 34 us  [correlate(): pl.pallas_call(functools.partial(correlate_kernel, uptime.shape[1]), out_...]
where the time goes in v3:
time: 52.9 us; the launch traced here: 52.6 us
  Pallas kernels  49.9 us (94%)
  local copies, waits for them, and re-layouts  1.47 us (3%)
  other arithmetic  1.3 us (2%)
    pallas_call x1, Pallas kernels, correlate(): pl.pallas_call(functools.partial(correlate_kernel, uptime.shape[1]), out_...  34 us
    pallas_call x1, Pallas kernels, reduce_scatter(): pl.pallas_call(functools.partial(reduce_kernel, x_size, z_size), out_shap...  15.8 us
    unnamed x1, local copies, waits for them, and re-layouts  1.47 us
    concatenate x1, other arithmetic, correlate(): counts = jnp.concatenate([moveouts.T, uptime.T], axis=0)  1.3 us

profile of v3, /device:TPU:0, one launch (start us, length us, event | category | flops | bytes accessed | tf_op | source)
XLA Modules:
  0.0 52.6 jit_solution(26921332991086032)
XLA Ops:
  0.0 1.3 %pad_add_fusion.counts = s32[5,16]{1,0:T(8,128)} fusion(s32[2,16]{1,0:T(2,128)} %bitcast.7, s32[3,16]{1,0:T(4,128)} %bitcast.6), kind=kLoop, calls=%fused_computation | loop fusion | flops 80 | bytes 640 | tf_op jit(solution)/shard_map/concatenate | solution.py:96
  1.3 34.0 %correlate.1.part = f32[1024,256]{1,0:T(8,128)} custom-call(s32[5,16]{1,0:T(8,128)} %pad_add_fusion.counts, bf16[3,16,1024]{2,1,0:T(8,128)(2,1)} %bitcast.5, bf16[16,3,200,256]{3,2,1,0:T(8,128)(2,1)} %templates.1), custom_call_target="tpu_custom_call" | custom-call | tf_op jit(solution)/shard_map/correlate/pallas_call | solution.py:97
  35.3 15.8 %reduce_scatter.1 = f32[64,256]{1,0:T(8,128)} custom-call(f32[1024,256]{1,0:T(8,128)} %correlate.1.part), custom_call_target="tpu_custom_call" | custom-call | tf_op jit(solution)/shard_map/reduce_scatter/pallas_call | solution.py:204
  51.2 1.5 %copy.6 = f32[256,64]{0,1:T(8,128)} copy(f32[256,64]{0,1:T(8,128)} %bitcast.4) | data formatting | bytes 131072
